TPU v7x, 32 devices: a whole 2x2x4 slice. The times are simulated.
32 devices in a mesh: patch: 8 (over z, core), visit: 4 (over y, x).
Axes of the slice: x: 2, y: 2, z: 4, core: 2. Of those that a mesh axis runs over, the one named last changes fastest.
Arguments:
- blocks: bfloat16 [8, 4, 16, 256, 256], P('patch', 'visit'), may hold values from -6 to 6
- block_patch: int32 [8, 4, 16, 1], P('patch', 'visit'), may hold values from 0 to 7; in each aligned block of 16 rows (0 to 15, 16 to 31, ..., all dimensions but the last counted through in order) at most 2 rows name the same one
- block_slot: int32 [8, 4, 16], P('patch', 'visit'), may hold values from 0 to 7
- block_count: int32 [8, 4], P('patch', 'visit'), may hold values from 12 to 16, as said below
- template: bfloat16 [8, 512, 1024], P('patch', 'visit'), may hold values from -6 to 6
- basis_rows: bfloat16 [9, 21], replicated, may hold values from -1.25 to 1.25
- basis_cols: float32 [9, 21], replicated, may hold values from -1.25 to 1.25
- coeffs: float32 [4, 9], P('visit'), may hold values from -2 to 2
- psf_rows: bfloat16 [4, 2, 25], P('visit'), may hold values from -1.25 to 1.25
- psf_cols: bfloat16 [4, 2, 25], P('visit'), may hold values from -1.25 to 1.25
Outputs:
- filtered: float32 [8, 4, 512, 1024], P('patch', 'visit')
Inputs may be any that keep to these rules, and one draw needn't show every extreme that they name: `block_patch`: among the 16 entries of one list (one patch index and visit) no patch is named more than 2 times, and some list names a patch exactly 2 times. Entries at positions block_count and beyond are unused.
All inputs are finite; a program needn't handle non-finite values.
Results may differ from a plain program's by a relative error of at most 0.005.
Values may be sent and summed in bfloat16 or wider, within the bound.
A program may use at most 128 MiB of HBM per device.

v0:
```python
import jax
import jax.numpy as jnp
from jax import lax
from jax.sharding import PartitionSpec as P

CAP = 2


def one_hot_bands(length, tile_size):
    band_shape = (3, length, tile_size, tile_size)
    side_ids = lax.broadcasted_iota(jnp.int32, band_shape, 0) - 1
    tap_ids = lax.broadcasted_iota(jnp.int32, band_shape, 1)
    inner = lax.broadcasted_iota(jnp.int32, band_shape, 2)
    outer = lax.broadcasted_iota(jnp.int32, band_shape, 3)
    return (side_ids * tile_size + inner - outer + length // 2 == tap_ids).astype(jnp.float32)


def band_tables(kernel_taps, one_hot):
    return jnp.einsum(
        "cl,dlij->cdij", kernel_taps.astype(jnp.float32), one_hot, precision=lax.Precision.HIGHEST
    ).astype(jnp.bfloat16)


def across_columns(source, tables):
    tile_size = tables.shape[-1]
    height, breadth = source.shape
    tile_count = breadth // tile_size
    tiled = source.reshape(height, tile_count, tile_size)
    zero_block = jnp.zeros((height, 1, tile_size), source.dtype)
    left_side = jnp.concatenate([zero_block, tiled[:, :-1]], axis=1)
    right_side = jnp.concatenate([tiled[:, 1:], zero_block], axis=1)
    summed = jnp.einsum("hbt,ctu->chbu", tiled, tables[:, 1], preferred_element_type=jnp.float32)
    summed = summed + jnp.einsum(
        "hbt,ctu->chbu", left_side, tables[:, 0], preferred_element_type=jnp.float32
    )
    summed = summed + jnp.einsum(
        "hbt,ctu->chbu", right_side, tables[:, 2], preferred_element_type=jnp.float32
    )
    return summed.reshape(tables.shape[0], height, breadth)


def across_rows(source, tables):
    tile_size = tables.shape[-1]
    channels, height, breadth = source.shape
    tile_count = height // tile_size
    tiled = source.reshape(channels, tile_count, tile_size, breadth)
    zero_block = jnp.zeros((channels, 1, tile_size, breadth), source.dtype)
    left_side = jnp.concatenate([zero_block, tiled[:, :-1]], axis=1)
    right_side = jnp.concatenate([tiled[:, 1:], zero_block], axis=1)
    summed = jnp.einsum("cbin,cij->bjn", tiled, tables[:, 1], preferred_element_type=jnp.float32)
    summed = summed + jnp.einsum(
        "cbin,cij->bjn", left_side, tables[:, 0], preferred_element_type=jnp.float32
    )
    summed = summed + jnp.einsum(
        "cbin,cij->bjn", right_side, tables[:, 2], preferred_element_type=jnp.float32
    )
    return summed.reshape(height, breadth)


def place_blocks(
    blocks, block_patch, block_slot, block_count, capacity, slot_total, height, breadth
):
    count_here = blocks.shape[2]
    block_edge = blocks.shape[3]
    pieces = blocks.reshape(count_here, block_edge * block_edge)
    destination = block_patch.reshape(count_here)
    slot_index = block_slot.reshape(count_here)
    row_order = lax.broadcasted_iota(jnp.int32, (count_here, count_here), 0)
    col_order = lax.broadcasted_iota(jnp.int32, (count_here, count_here), 1)
    same_patch = destination[:, None] == destination[None, :]
    earlier = jnp.sum((same_patch & (col_order < row_order)).astype(jnp.int32), axis=1)
    target = destination * capacity + earlier
    live_mask = lax.iota(jnp.int32, count_here) < block_count.reshape(())
    n_patch = lax.axis_size("patch")
    places = n_patch * capacity
    place_ids = lax.broadcasted_iota(jnp.int32, (places, count_here), 0)
    picker = ((place_ids == target[None, :]) & live_mask[None, :]).astype(jnp.float32)
    outgoing = jnp.dot(
        picker.astype(jnp.bfloat16), pieces, preferred_element_type=jnp.float32
    ).astype(jnp.bfloat16)
    outgoing = outgoing.reshape(n_patch, capacity, block_edge * block_edge)
    labels = (
        jnp.dot(
            picker, (slot_index - slot_total).astype(jnp.float32), precision=lax.Precision.HIGHEST
        )
        + slot_total
    )
    labels = labels.astype(jnp.bfloat16).reshape(n_patch, capacity)
    arrived, arrived_slots = (
        lax.all_to_all(outgoing, "patch", split_axis=0, concat_axis=0, tiled=True),
        lax.all_to_all(labels, "patch", split_axis=0, concat_axis=0, tiled=True),
    )
    arrived = arrived.reshape(places, block_edge * block_edge)
    slot_ids = lax.broadcasted_iota(jnp.float32, (slot_total, places), 0)
    chosen = (slot_ids == arrived_slots.reshape(1, places).astype(jnp.float32)).astype(jnp.bfloat16)
    placed = jnp.dot(chosen, arrived, preferred_element_type=jnp.float32)
    tall_count = height // block_edge
    wide_count = breadth // block_edge
    placed = placed.reshape(tall_count, wide_count, block_edge, block_edge).transpose(0, 2, 1, 3)
    return placed.reshape(height, breadth)


def per_device(
    blocks,
    block_patch,
    block_slot,
    block_count,
    template,
    basis_rows,
    basis_cols,
    coeffs,
    psf_rows,
    psf_cols,
):
    local_rows = template.shape[1]
    breadth = template.shape[2]
    height = local_rows * lax.axis_size("visit")
    block_edge = blocks.shape[3]
    slot_total = height // block_edge * (breadth // block_edge)
    science = place_blocks(
        blocks, block_patch, block_slot, block_count, CAP, slot_total, height, breadth
    )
    column_hot = one_hot_bands(basis_rows.shape[1], min(128, breadth))
    row_hot = one_hot_bands(basis_cols.shape[1], min(128, height))
    scaled = (coeffs[0][:, None] * basis_cols).astype(jnp.bfloat16)
    start_image = jnp.zeros((height, breadth), jnp.float32)
    all_tables = band_tables(basis_rows, column_hot)
    partial_rows = across_columns(template[0], all_tables).astype(jnp.bfloat16)
    smoothed_all = lax.all_gather(partial_rows, "visit", axis=1, tiled=True)

    def per_stack(model_image, profiles):
        smoothed, col_taps = profiles
        col_table = band_tables(col_taps[None], row_hot)
        return (model_image + across_rows(smoothed[None], col_table), None)

    model_image = lax.scan(per_stack, start_image, (smoothed_all, scaled))[0]
    difference = (science - model_image).astype(jnp.bfloat16)
    psf_column_hot = one_hot_bands(psf_rows.shape[2], min(128, breadth))
    psf_row_hot = one_hot_bands(psf_cols.shape[2], min(128, height))
    blurred = across_columns(difference, band_tables(psf_rows[0], psf_column_hot)).astype(
        jnp.bfloat16
    )
    filtered = across_rows(blurred, band_tables(psf_cols[0], psf_row_hot))
    return filtered[None, None]


def solution(mesh):
    placed = (
        P("patch", "visit", None, None, None),
        P("patch", "visit", None, None),
        P("patch", "visit", None),
        P("patch", "visit"),
        P("patch", "visit", None),
        P(),
        P(),
        P("visit", None),
        P("visit", None, None),
        P("visit", None, None),
    )
    return jax.shard_map(
        per_device,
        mesh=mesh,
        in_specs=placed,
        out_specs=P("patch", "visit", None, None),
        check_vma=False,
    )
```

profile of v0, /device:TPU:0, one launch (start us, length us, event | category | flops | bytes accessed | tf_op | source)
XLA Modules:
  0.0 238.5 jit_solution(14624126274584516626)
XLA Ops:
  16.9 6.4 %all-to-all-start = ((bf16[8,1,2]{2,1,0:T(2,128)(2,1)}), bf16[8,1,2]{2,1,0:T(2,128)(2,1)S(1)}, u32[]{:S(2)}, u32[]{:S(2)}) async-start(bf16[8,1,2]{2,1,0:T(2,128)(2,1)} %all_to_all.12), calls=%async_computation | async-start | bytes 8192 | tf_op jit(solution)/shard_map/all_to_all | solution.py:91
  28.8 4.5 %all-to-all-start.1 = ((bf16[8,2,65536]{2,1,0:T(2,128)(2,1)}), bf16[8,2,65536]{2,1,0:T(2,128)(2,1)}, u32[]{:S(2)}, u32[]{:S(2)}) async-start(bf16[8,2,65536]{2,1,0:T(2,128)(2,1)} %reshape.116), calls=%async_computation.1 | async-start | bytes 4194304 | tf_op jit(solution)/shard_map/all_to_all | solution.py:90
  37.3 44.9 %all-to-all-done.1 = bf16[8,2,65536]{2,1,0:T(2,128)(2,1)} async-done(((bf16[8,2,65536]{2,1,0:T(2,128)(2,1)}), bf16[8,2,65536]{2,1,0:T(2,128)(2,1)}, u32[]{:S(2)}, u32[]{:S(2)}) %all-to-all-start.1) | async-done | bytes 2097184 | tf_op jit(solution)/shard_map/all_to_all | solution.py:90
  87.1 27.0 %all-gather.2.cloned.1.call-done = bf16[9,512,1024]{2,1,0:T(8,128)(2,1)} async-done(((bf16[9,128,1024]{2,1,0:T(8,128)(2,1)}), bf16[9,512,1024]{2,1,0:T(8,128)(2,1)}) %all-gather.2.cloned.1.call-update) | async-done | bytes 9437200 | tf_op jit(solution)/shard_map/all_gather | solution.py:129
  114.1 97.7 %while.11 = (s32[]{:T(128)}, f32[512,1024]{1,0:T(8,128)}, bf16[9,21]{1,0:T(8,128)(2,1)S(1)}, bf16[9,512,1024]{2,1,0:T(8,128)(2,1)}, s32[3]{0:T(128)S(1)}, /*index=5*/s32[]{:T(128)}, s32[]{:T(128)}) while((s32[]{:T(128)}, f32[512,1024]{1,0:T(8,128)}, bf16[9,21]{1,0:T(8,128)(2,1)S(1)}, bf16[9,512,1024]{2,1,0:T(8,128)(2,1)}, ...), condition=%wide.region_2.3_spmd.clone, body=%wide.region_1.2_spmd.clone.sunk | while | flops 422297600 | bytes 33489512 | solution.py:136
  114.7 4.0 %fusion.117 = bf16[1,3,128,128]{3,0,2,1:T(2,128)(2,1)S(1)} fusion(f32[3,21,128,128]{3,2,1,0:T(8,128)S(1)} %fusion.116, bf16[9,21]{1,0:T(8,128)(2,1)S(1)} %get-tuple-element.132, s32[]{:T(128)} %get-tuple-element.123), kind=kOutput, calls=%fused_computation.1.clone.1 | convolution fusion | flops 12386304 | bytes 4227588 | tf_op jit(solution)/shard_map/while/body/eval_jaxpr/cl,dlij->cdij/dot_general | solution.py:19
  124.1 4.0 %fusion.117 = bf16[1,3,128,128]{3,0,2,1:T(2,128)(2,1)S(1)} fusion(f32[3,21,128,128]{3,2,1,0:T(8,128)S(1)} %fusion.116, bf16[9,21]{1,0:T(8,128)(2,1)S(1)} %get-tuple-element.132, s32[]{:T(128)} %get-tuple-element.123), kind=kOutput, calls=%fused_computation.1.clone.1 | convolution fusion | flops 12386304 | bytes 4227588 | tf_op jit(solution)/shard_map/while/body/eval_jaxpr/cl,dlij->cdij/dot_general | solution.py:19
  131.0 3.6 %bitcast_add_fusion.4 = f32[512,1024]{1,0:T(8,128)} fusion(f32[128,4,1024]{2,0,1:T(8,128)S(1)} %add_add_fusion.2, f32[512,1024]{1,0:T(8,128)} %get-tuple-element.124, pred[]{:T(512)S(6)} %compare.11), kind=kLoop, calls=%fused_computation.5.clone.1 | loop fusion | flops 1048576 | bytes 6291457 | tf_op jit(solution)/shard_map/while/body/eval_jaxpr/add | solution.py:134
  135.2 4.0 %fusion.117 = bf16[1,3,128,128]{3,0,2,1:T(2,128)(2,1)S(1)} fusion(f32[3,21,128,128]{3,2,1,0:T(8,128)S(1)} %fusion.116, bf16[9,21]{1,0:T(8,128)(2,1)S(1)} %get-tuple-element.132, s32[]{:T(128)} %get-tuple-element.123), kind=kOutput, calls=%fused_computation.1.clone.1 | convolution fusion | flops 12386304 | bytes 4227588 | tf_op jit(solution)/shard_map/while/body/eval_jaxpr/cl,dlij->cdij/dot_general | solution.py:19
  142.0 3.6 %bitcast_add_fusion.4 = f32[512,1024]{1,0:T(8,128)} fusion(f32[128,4,1024]{2,0,1:T(8,128)S(1)} %add_add_fusion.2, f32[512,1024]{1,0:T(8,128)} %get-tuple-element.124, pred[]{:T(512)S(6)} %compare.11), kind=kLoop, calls=%fused_computation.5.clone.1 | loop fusion | flops 1048576 | bytes 6291457 | tf_op jit(solution)/shard_map/while/body/eval_jaxpr/add | solution.py:134
  146.2 4.0 %fusion.117 = bf16[1,3,128,128]{3,0,2,1:T(2,128)(2,1)S(1)} fusion(f32[3,21,128,128]{3,2,1,0:T(8,128)S(1)} %fusion.116, bf16[9,21]{1,0:T(8,128)(2,1)S(1)} %get-tuple-element.132, s32[]{:T(128)} %get-tuple-element.123), kind=kOutput, calls=%fused_computation.1.clone.1 | convolution fusion | flops 12386304 | bytes 4227588 | tf_op jit(solution)/shard_map/while/body/eval_jaxpr/cl,dlij->cdij/dot_general | solution.py:19
  153.1 3.6 %bitcast_add_fusion.4 = f32[512,1024]{1,0:T(8,128)} fusion(f32[128,4,1024]{2,0,1:T(8,128)S(1)} %add_add_fusion.2, f32[512,1024]{1,0:T(8,128)} %get-tuple-element.124, pred[]{:T(512)S(6)} %compare.11), kind=kLoop, calls=%fused_computation.5.clone.1 | loop fusion | flops 1048576 | bytes 6291457 | tf_op jit(solution)/shard_map/while/body/eval_jaxpr/add | solution.py:134
  157.2 4.0 %fusion.117 = bf16[1,3,128,128]{3,0,2,1:T(2,128)(2,1)S(1)} fusion(f32[3,21,128,128]{3,2,1,0:T(8,128)S(1)} %fusion.116, bf16[9,21]{1,0:T(8,128)(2,1)S(1)} %get-tuple-element.132, s32[]{:T(128)} %get-tuple-element.123), kind=kOutput, calls=%fused_computation.1.clone.1 | convolution fusion | flops 12386304 | bytes 4227588 | tf_op jit(solution)/shard_map/while/body/eval_jaxpr/cl,dlij->cdij/dot_general | solution.py:19
  164.1 3.6 %bitcast_add_fusion.4 = f32[512,1024]{1,0:T(8,128)} fusion(f32[128,4,1024]{2,0,1:T(8,128)S(1)} %add_add_fusion.2, f32[512,1024]{1,0:T(8,128)} %get-tuple-element.124, pred[]{:T(512)S(6)} %compare.11), kind=kLoop, calls=%fused_computation.5.clone.1 | loop fusion | flops 1048576 | bytes 6291457 | tf_op jit(solution)/shard_map/while/body/eval_jaxpr/add | solution.py:134
  168.3 4.0 %fusion.117 = bf16[1,3,128,128]{3,0,2,1:T(2,128)(2,1)S(1)} fusion(f32[3,21,128,128]{3,2,1,0:T(8,128)S(1)} %fusion.116, bf16[9,21]{1,0:T(8,128)(2,1)S(1)} %get-tuple-element.132, s32[]{:T(128)} %get-tuple-element.123), kind=kOutput, calls=%fused_computation.1.clone.1 | convolution fusion | flops 12386304 | bytes 4227588 | tf_op jit(solution)/shard_map/while/body/eval_jaxpr/cl,dlij->cdij/dot_general | solution.py:19
  175.1 3.6 %bitcast_add_fusion.4 = f32[512,1024]{1,0:T(8,128)} fusion(f32[128,4,1024]{2,0,1:T(8,128)S(1)} %add_add_fusion.2, f32[512,1024]{1,0:T(8,128)} %get-tuple-element.124, pred[]{:T(512)S(6)} %compare.11), kind=kLoop, calls=%fused_computation.5.clone.1 | loop fusion | flops 1048576 | bytes 6291457 | tf_op jit(solution)/shard_map/while/body/eval_jaxpr/add | solution.py:134
  179.3 4.0 %fusion.117 = bf16[1,3,128,128]{3,0,2,1:T(2,128)(2,1)S(1)} fusion(f32[3,21,128,128]{3,2,1,0:T(8,128)S(1)} %fusion.116, bf16[9,21]{1,0:T(8,128)(2,1)S(1)} %get-tuple-element.132, s32[]{:T(128)} %get-tuple-element.123), kind=kOutput, calls=%fused_computation.1.clone.1 | convolution fusion | flops 12386304 | bytes 4227588 | tf_op jit(solution)/shard_map/while/body/eval_jaxpr/cl,dlij->cdij/dot_general | solution.py:19
  186.2 3.6 %bitcast_add_fusion.4 = f32[512,1024]{1,0:T(8,128)} fusion(f32[128,4,1024]{2,0,1:T(8,128)S(1)} %add_add_fusion.2, f32[512,1024]{1,0:T(8,128)} %get-tuple-element.124, pred[]{:T(512)S(6)} %compare.11), kind=kLoop, calls=%fused_computation.5.clone.1 | loop fusion | flops 1048576 | bytes 6291457 | tf_op jit(solution)/shard_map/while/body/eval_jaxpr/add | solution.py:134
  190.3 4.0 %fusion.117 = bf16[1,3,128,128]{3,0,2,1:T(2,128)(2,1)S(1)} fusion(f32[3,21,128,128]{3,2,1,0:T(8,128)S(1)} %fusion.116, bf16[9,21]{1,0:T(8,128)(2,1)S(1)} %get-tuple-element.132, s32[]{:T(128)} %get-tuple-element.123), kind=kOutput, calls=%fused_computation.1.clone.1 | convolution fusion | flops 12386304 | bytes 4227588 | tf_op jit(solution)/shard_map/while/body/eval_jaxpr/cl,dlij->cdij/dot_general | solution.py:19
  197.2 3.6 %bitcast_add_fusion.4 = f32[512,1024]{1,0:T(8,128)} fusion(f32[128,4,1024]{2,0,1:T(8,128)S(1)} %add_add_fusion.2, f32[512,1024]{1,0:T(8,128)} %get-tuple-element.124, pred[]{:T(512)S(6)} %compare.11), kind=kLoop, calls=%fused_computation.5.clone.1 | loop fusion | flops 1048576 | bytes 6291457 | tf_op jit(solution)/shard_map/while/body/eval_jaxpr/add | solution.py:134
  201.4 4.0 %fusion.117 = bf16[1,3,128,128]{3,0,2,1:T(2,128)(2,1)S(1)} fusion(f32[3,21,128,128]{3,2,1,0:T(8,128)S(1)} %fusion.116, bf16[9,21]{1,0:T(8,128)(2,1)S(1)} %get-tuple-element.132, s32[]{:T(128)} %get-tuple-element.123), kind=kOutput, calls=%fused_computation.1.clone.1 | convolution fusion | flops 12386304 | bytes 4227588 | tf_op jit(solution)/shard_map/while/body/eval_jaxpr/cl,dlij->cdij/dot_general | solution.py:19
  208.2 3.6 %bitcast_add_fusion.4 = f32[512,1024]{1,0:T(8,128)} fusion(f32[128,4,1024]{2,0,1:T(8,128)S(1)} %add_add_fusion.2, f32[512,1024]{1,0:T(8,128)} %get-tuple-element.124, pred[]{:T(512)S(6)} %compare.11), kind=kLoop, calls=%fused_computation.5.clone.1 | loop fusion | flops 1048576 | bytes 6291457 | tf_op jit(solution)/shard_map/while/body/eval_jaxpr/add | solution.py:134
  211.8 3.0 %copy.82 = f32[512,1024]{0,1:T(8,128)} copy(f32[512,1024]{1,0:T(8,128)} %get-tuple-element.32) | data formatting | bytes 4194304 | tf_op jit(solution)/shard_map/while | solution.py:136
  225.5 3.0 %copy.90 = bf16[2,4,128,1024]{3,2,0,1:T(8,128)(2,1)S(1)} copy(bf16[2,4,128,1024]{2,1,3,0:T(4,128)(2,1)} %convert_element_type.117) | data formatting | bytes 4194304 | tf_op jit(solution)/shard_map/convert_element_type | solution.py:140
  (147 shorter events, 70.6 us)
Async XLA Ops:
  6.5 0.7 copy-start
  6.5 107.6 %all-gather.2.cloned.1.call-start = ((), (), s32[]{:S(2)}) async-start(), calls=%async_computation.2 | async-start | bytes 11796480 | tf_op jit(solution)/shard_map/all_gather | solution.py:129
  8.6 1.0 copy-start.5
  15.0 0.8 copy-start.8
  15.0 1.0 copy-start.9
  15.0 8.2 %copy-start.4 = (bf16[1,1,16,256,256]{4,3,2,1,0:T(8,128)(2,1)S(1)}, bf16[1,1,16,256,256]{4,3,2,1,0:T(8,128)(2,1)}, u32[]{:S(2)}) copy-start(bf16[1,1,16,256,256]{4,3,2,1,0:T(8,128)(2,1)} %param.12) | copy-start | bytes 6291460
  16.9 11.9 %all-to-all-start = ((bf16[8,1,2]{2,1,0:T(2,128)(2,1)}), bf16[8,1,2]{2,1,0:T(2,128)(2,1)S(1)}, u32[]{:S(2)}, u32[]{:S(2)}) async-start(bf16[8,1,2]{2,1,0:T(2,128)(2,1)} %all_to_all.12), calls=%async_computation | async-start | bytes 8192 | tf_op jit(solution)/shard_map/all_to_all | solution.py:91
  27.4 5.9 %copy-start.10 = (bf16[1,2,25]{2,1,0:T(2,128)(2,1)S(1)}, bf16[1,2,25]{2,1,0:T(2,128)(2,1)}, u32[]{:S(2)}) copy-start(bf16[1,2,25]{2,1,0:T(2,128)(2,1)} %param.21) | copy-start | bytes 304
  28.8 53.4 %all-to-all-start.1 = ((bf16[8,2,65536]{2,1,0:T(2,128)(2,1)}), bf16[8,2,65536]{2,1,0:T(2,128)(2,1)}, u32[]{:S(2)}, u32[]{:S(2)}) async-start(bf16[8,2,65536]{2,1,0:T(2,128)(2,1)} %reshape.116), calls=%async_computation.1 | async-start | bytes 4194304 | tf_op jit(solution)/shard_map/all_to_all | solution.py:90
  33.3 2.1 copy-start.6
  33.4 2.1 copy-start.7
  33.4 2.1 copy-start.11
  211.8 3.0 %copy-start.2 = (f32[512,1024]{0,1:T(8,128)S(1)}, f32[512,1024]{0,1:T(8,128)}, u32[]{:S(2)}) copy-start(f32[512,1024]{0,1:T(8,128)} %copy.81) | copy-start | bytes 6291460
  221.5 1.2 copy-start.3
  229.8 1.9 copy-start.1
Sparse Core Ops, SparseCore 0:
  15.1 98.9 all-gather.1
where the time goes:
time: 240 us; the launch traced here: 239 us
  waiting for transfers between devices  73.3 us (31%)
  matrix products  59.7 us (25%)
  local copies, waits for them, and re-layouts  41.5 us (17%)
  other arithmetic  38.2 us (16%)
  between operations  14.5 us (6%)
  starting transfers between devices  10.9 us (5%)
    all_to_all x1, waiting for transfers between devices, place_blocks(): lax.all_to_all(outgoing, 'patch', split_axis=0, concat_axis=0, tiled=True)  44.9 us
    dot_general x12, matrix products, band_tables(): jnp.einsum('cl,dlij->cdij', kernel_taps.astype(jnp.float32), one_hot, pre...  39.9 us
    add x9, other arithmetic, per_stack(): return (model_image + across_rows(smoothed[None], col_table), None)  30.6 us
    all_gather x1, waiting for transfers between devices, per_device(): smoothed_all = lax.all_gather(partial_rows, 'visit', axis=1, tiled=True)  27 us
    dynamic_slice x9, local copies, waits for them, and re-layouts, per_device(): model_image = lax.scan(per_stack, start_image, (smoothed_all, scaled))[0]  11.7 us
    unnamed x31, local copies, waits for them, and re-layouts  6.85 us
    all_to_all x1, starting transfers between devices, place_blocks(): lax.all_to_all(labels, 'patch', split_axis=0, concat_axis=0, tiled=True)  6.35 us
    dot_general x10, matrix products, across_rows(): jnp.einsum('cbin,cij->bjn', left_side, tables[:, 0], preferred_element_ty...  5.32 us
  transfers between devices with their start and end apart: 3, of which 3 were waited for; matrix products, arithmetic and copies ran while one was open for 6% of the time, Pallas kernels for 0%

commit v1 on v0

--- a/solution.py
+++ b/solution.py
@@ -126,7 +126,7 @@
     start_image = jnp.zeros((height, breadth), jnp.float32)
     all_tables = band_tables(basis_rows, column_hot)
     partial_rows = across_columns(template[0], all_tables).astype(jnp.bfloat16)
-    smoothed_all = lax.all_gather(partial_rows, "visit", axis=1, tiled=True)
+    smoothed_all = jnp.concatenate(lax.all_gather(partial_rows, "visit"), axis=1)
 
     def per_stack(model_image, profiles):
         smoothed, col_taps = profiles

time: 240 us -> 248 us (1.033)
  local copies, waits for them, and re-layouts: 41.5 us -> 50.7 us
    all_gather x0 -> x1, local copies, waits for them, and re-layouts: none -> 9.22 us  [per_device(): lax.all_gather(partial_rows, 'visit')]
  transfers between devices with their start and end apart: 3 -> 3, of which waited for: 3 -> 3; matrix products, arithmetic and copies ran while one was open for 6% -> 5% of each run, Pallas kernels for 0% -> 0%
where the time goes in v1:
time: 248 us; the launch traced here: 247 us
  waiting for transfers between devices  73.2 us (30%)
  matrix products  59.7 us (24%)
  local copies, waits for them, and re-layouts  50.7 us (20%)
  other arithmetic  37.4 us (15%)
  between operations  14.5 us (6%)
  starting transfers between devices  10.9 us (4%)
    all_to_all x1, waiting for transfers between devices, place_blocks(): lax.all_to_all(outgoing, 'patch', split_axis=0, concat_axis=0, tiled=True)  44.9 us
    dot_general x12, matrix products, band_tables(): jnp.einsum('cl,dlij->cdij', kernel_taps.astype(jnp.float32), one_hot, pre...  39.9 us
    add x9, other arithmetic, per_stack(): return (model_image + across_rows(smoothed[None], col_table), None)  29.8 us
    all_gather x1, waiting for transfers between devices, per_device(): lax.all_gather(partial_rows, 'visit')  26.9 us
    dynamic_slice x9, local copies, waits for them, and re-layouts, per_device(): model_image = lax.scan(per_stack, start_image, (smoothed_all, scaled))[0]  11.7 us
    all_gather x1, local copies, waits for them, and re-layouts, per_device(): lax.all_gather(partial_rows, 'visit')  9.22 us
    unnamed x31, local copies, waits for them, and re-layouts  6.84 us
    all_to_all x1, starting transfers between devices, place_blocks(): lax.all_to_all(labels, 'patch', split_axis=0, concat_axis=0, tiled=True)  6.35 us
  transfers between devices with their start and end apart: 3, of which 3 were waited for; matrix products, arithmetic and copies ran while one was open for 5% of the time, Pallas kernels for 0%

profile of v1, /device:TPU:0, one launch (start us, length us, event | category | flops | bytes accessed | tf_op | source)
XLA Modules:
  0.0 247.0 jit_solution(3087709217008129473)
XLA Ops:
  16.9 6.4 %all-to-all-start = ((bf16[8,1,2]{2,1,0:T(2,128)(2,1)}), bf16[8,1,2]{2,1,0:T(2,128)(2,1)S(1)}, u32[]{:S(2)}, u32[]{:S(2)}) async-start(bf16[8,1,2]{2,1,0:T(2,128)(2,1)} %all_to_all.12), calls=%async_computation | async-start | bytes 8192 | tf_op jit(solution)/shard_map/all_to_all | solution.py:91
  28.8 4.5 %all-to-all-start.1 = ((bf16[8,2,65536]{2,1,0:T(2,128)(2,1)}), bf16[8,2,65536]{2,1,0:T(2,128)(2,1)}, u32[]{:S(2)}, u32[]{:S(2)}) async-start(bf16[8,2,65536]{2,1,0:T(2,128)(2,1)} %reshape.132), calls=%async_computation.1 | async-start | bytes 4194304 | tf_op jit(solution)/shard_map/all_to_all | solution.py:90
  37.3 44.9 %all-to-all-done.1 = bf16[8,2,65536]{2,1,0:T(2,128)(2,1)} async-done(((bf16[8,2,65536]{2,1,0:T(2,128)(2,1)}), bf16[8,2,65536]{2,1,0:T(2,128)(2,1)}, u32[]{:S(2)}, u32[]{:S(2)}) %all-to-all-start.1) | async-done | bytes 2097184 | tf_op jit(solution)/shard_map/all_to_all | solution.py:90
  87.2 26.9 %all-gather.2.cloned.1.call-done = bf16[4,9,128,1024]{3,2,1,0:T(8,128)(2,1)} async-done(((bf16[1,9,128,1024]{3,2,1,0:T(8,128)(2,1)}), bf16[4,9,128,1024]{3,2,1,0:T(8,128)(2,1)}) %all-gather.2.cloned.1.call-update) | async-done | bytes 9437200 | tf_op jit(solution)/shard_map/all_gather | solution.py:129
  114.1 9.2 %copy.106 = bf16[4,9,128,1024]{3,2,0,1:T(8,128)(2,1)} copy(bf16[4,9,128,1024]{3,2,1,0:T(8,128)(2,1)} %all-gather.2.cloned.1.call-done) | data formatting | bytes 18874368 | tf_op jit(solution)/shard_map/all_gather | solution.py:129
  123.3 96.9 %while.11 = (s32[]{:T(128)}, f32[512,1024]{1,0:T(8,128)}, bf16[9,21]{1,0:T(8,128)(2,1)S(1)}, bf16[9,512,1024]{2,1,0:T(8,128)(2,1)}, s32[3]{0:T(128)S(1)}, /*index=5*/s32[]{:T(128)}, s32[]{:T(128)}) while((s32[]{:T(128)}, f32[512,1024]{1,0:T(8,128)}, bf16[9,21]{1,0:T(8,128)(2,1)S(1)}, bf16[9,512,1024]{2,1,0:T(8,128)(2,1)}, ...), condition=%wide.region_2.3_spmd.clone, body=%wide.region_1.2_spmd.clone.sunk | while | flops 422297600 | bytes 33489512 | solution.py:136
  123.9 4.0 %fusion.117 = bf16[1,3,128,128]{3,0,2,1:T(2,128)(2,1)S(1)} fusion(f32[3,21,128,128]{3,2,1,0:T(8,128)S(1)} %fusion.116, bf16[9,21]{1,0:T(8,128)(2,1)S(1)} %get-tuple-element.132, s32[]{:T(128)} %get-tuple-element.123), kind=kOutput, calls=%fused_computation.1.clone.1 | convolution fusion | flops 12386304 | bytes 4227588 | tf_op jit(solution)/shard_map/while/body/eval_jaxpr/cl,dlij->cdij/dot_general | solution.py:19
  133.3 4.0 %fusion.117 = bf16[1,3,128,128]{3,0,2,1:T(2,128)(2,1)S(1)} fusion(f32[3,21,128,128]{3,2,1,0:T(8,128)S(1)} %fusion.116, bf16[9,21]{1,0:T(8,128)(2,1)S(1)} %get-tuple-element.132, s32[]{:T(128)} %get-tuple-element.123), kind=kOutput, calls=%fused_computation.1.clone.1 | convolution fusion | flops 12386304 | bytes 4227588 | tf_op jit(solution)/shard_map/while/body/eval_jaxpr/cl,dlij->cdij/dot_general | solution.py:19
  140.1 3.5 %bitcast_add_fusion.4 = f32[512,1024]{1,0:T(8,128)} fusion(f32[128,4,1024]{2,0,1:T(8,128)S(1)} %add_add_fusion.2, f32[512,1024]{1,0:T(8,128)} %get-tuple-element.124, pred[]{:T(512)S(6)} %compare.11), kind=kLoop, calls=%fused_computation.5.clone.1 | loop fusion | flops 1048576 | bytes 6291457 | tf_op jit(solution)/shard_map/while/body/eval_jaxpr/add | solution.py:134
  144.2 4.0 %fusion.117 = bf16[1,3,128,128]{3,0,2,1:T(2,128)(2,1)S(1)} fusion(f32[3,21,128,128]{3,2,1,0:T(8,128)S(1)} %fusion.116, bf16[9,21]{1,0:T(8,128)(2,1)S(1)} %get-tuple-element.132, s32[]{:T(128)} %get-tuple-element.123), kind=kOutput, calls=%fused_computation.1.clone.1 | convolution fusion | flops 12386304 | bytes 4227588 | tf_op jit(solution)/shard_map/while/body/eval_jaxpr/cl,dlij->cdij/dot_general | solution.py:19
  151.1 3.5 %bitcast_add_fusion.4 = f32[512,1024]{1,0:T(8,128)} fusion(f32[128,4,1024]{2,0,1:T(8,128)S(1)} %add_add_fusion.2, f32[512,1024]{1,0:T(8,128)} %get-tuple-element.124, pred[]{:T(512)S(6)} %compare.11), kind=kLoop, calls=%fused_computation.5.clone.1 | loop fusion | flops 1048576 | bytes 6291457 | tf_op jit(solution)/shard_map/while/body/eval_jaxpr/add | solution.py:134
  155.2 4.0 %fusion.117 = bf16[1,3,128,128]{3,0,2,1:T(2,128)(2,1)S(1)} fusion(f32[3,21,128,128]{3,2,1,0:T(8,128)S(1)} %fusion.116, bf16[9,21]{1,0:T(8,128)(2,1)S(1)} %get-tuple-element.132, s32[]{:T(128)} %get-tuple-element.123), kind=kOutput, calls=%fused_computation.1.clone.1 | convolution fusion | flops 12386304 | bytes 4227588 | tf_op jit(solution)/shard_map/while/body/eval_jaxpr/cl,dlij->cdij/dot_general | solution.py:19
  162.0 3.5 %bitcast_add_fusion.4 = f32[512,1024]{1,0:T(8,128)} fusion(f32[128,4,1024]{2,0,1:T(8,128)S(1)} %add_add_fusion.2, f32[512,1024]{1,0:T(8,128)} %get-tuple-element.124, pred[]{:T(512)S(6)} %compare.11), kind=kLoop, calls=%fused_computation.5.clone.1 | loop fusion | flops 1048576 | bytes 6291457 | tf_op jit(solution)/shard_map/while/body/eval_jaxpr/add | solution.py:134
  166.1 4.0 %fusion.117 = bf16[1,3,128,128]{3,0,2,1:T(2,128)(2,1)S(1)} fusion(f32[3,21,128,128]{3,2,1,0:T(8,128)S(1)} %fusion.116, bf16[9,21]{1,0:T(8,128)(2,1)S(1)} %get-tuple-element.132, s32[]{:T(128)} %get-tuple-element.123), kind=kOutput, calls=%fused_computation.1.clone.1 | convolution fusion | flops 12386304 | bytes 4227588 | tf_op jit(solution)/shard_map/while/body/eval_jaxpr/cl,dlij->cdij/dot_general | solution.py:19
  173.0 3.5 %bitcast_add_fusion.4 = f32[512,1024]{1,0:T(8,128)} fusion(f32[128,4,1024]{2,0,1:T(8,128)S(1)} %add_add_fusion.2, f32[512,1024]{1,0:T(8,128)} %get-tuple-element.124, pred[]{:T(512)S(6)} %compare.11), kind=kLoop, calls=%fused_computation.5.clone.1 | loop fusion | flops 1048576 | bytes 6291457 | tf_op jit(solution)/shard_map/while/body/eval_jaxpr/add | solution.py:134
  177.1 4.0 %fusion.117 = bf16[1,3,128,128]{3,0,2,1:T(2,128)(2,1)S(1)} fusion(f32[3,21,128,128]{3,2,1,0:T(8,128)S(1)} %fusion.116, bf16[9,21]{1,0:T(8,128)(2,1)S(1)} %get-tuple-element.132, s32[]{:T(128)} %get-tuple-element.123), kind=kOutput, calls=%fused_computation.1.clone.1 | convolution fusion | flops 12386304 | bytes 4227588 | tf_op jit(solution)/shard_map/while/body/eval_jaxpr/cl,dlij->cdij/dot_general | solution.py:19
  183.9 3.5 %bitcast_add_fusion.4 = f32[512,1024]{1,0:T(8,128)} fusion(f32[128,4,1024]{2,0,1:T(8,128)S(1)} %add_add_fusion.2, f32[512,1024]{1,0:T(8,128)} %get-tuple-element.124, pred[]{:T(512)S(6)} %compare.11), kind=kLoop, calls=%fused_computation.5.clone.1 | loop fusion | flops 1048576 | bytes 6291457 | tf_op jit(solution)/shard_map/while/body/eval_jaxpr/add | solution.py:134
  188.0 4.0 %fusion.117 = bf16[1,3,128,128]{3,0,2,1:T(2,128)(2,1)S(1)} fusion(f32[3,21,128,128]{3,2,1,0:T(8,128)S(1)} %fusion.116, bf16[9,21]{1,0:T(8,128)(2,1)S(1)} %get-tuple-element.132, s32[]{:T(128)} %get-tuple-element.123), kind=kOutput, calls=%fused_computation.1.clone.1 | convolution fusion | flops 12386304 | bytes 4227588 | tf_op jit(solution)/shard_map/while/body/eval_jaxpr/cl,dlij->cdij/dot_general | solution.py:19
  194.9 3.5 %bitcast_add_fusion.4 = f32[512,1024]{1,0:T(8,128)} fusion(f32[128,4,1024]{2,0,1:T(8,128)S(1)} %add_add_fusion.2, f32[512,1024]{1,0:T(8,128)} %get-tuple-element.124, pred[]{:T(512)S(6)} %compare.11), kind=kLoop, calls=%fused_computation.5.clone.1 | loop fusion | flops 1048576 | bytes 6291457 | tf_op jit(solution)/shard_map/while/body/eval_jaxpr/add | solution.py:134
  198.9 4.0 %fusion.117 = bf16[1,3,128,128]{3,0,2,1:T(2,128)(2,1)S(1)} fusion(f32[3,21,128,128]{3,2,1,0:T(8,128)S(1)} %fusion.116, bf16[9,21]{1,0:T(8,128)(2,1)S(1)} %get-tuple-element.132, s32[]{:T(128)} %get-tuple-element.123), kind=kOutput, calls=%fused_computation.1.clone.1 | convolution fusion | flops 12386304 | bytes 4227588 | tf_op jit(solution)/shard_map/while/body/eval_jaxpr/cl,dlij->cdij/dot_general | solution.py:19
  205.8 3.5 %bitcast_add_fusion.4 = f32[512,1024]{1,0:T(8,128)} fusion(f32[128,4,1024]{2,0,1:T(8,128)S(1)} %add_add_fusion.2, f32[512,1024]{1,0:T(8,128)} %get-tuple-element.124, pred[]{:T(512)S(6)} %compare.11), kind=kLoop, calls=%fused_computation.5.clone.1 | loop fusion | flops 1048576 | bytes 6291457 | tf_op jit(solution)/shard_map/while/body/eval_jaxpr/add | solution.py:134
  209.9 4.0 %fusion.117 = bf16[1,3,128,128]{3,0,2,1:T(2,128)(2,1)S(1)} fusion(f32[3,21,128,128]{3,2,1,0:T(8,128)S(1)} %fusion.116, bf16[9,21]{1,0:T(8,128)(2,1)S(1)} %get-tuple-element.132, s32[]{:T(128)} %get-tuple-element.123), kind=kOutput, calls=%fused_computation.1.clone.1 | convolution fusion | flops 12386304 | bytes 4227588 | tf_op jit(solution)/shard_map/while/body/eval_jaxpr/cl,dlij->cdij/dot_general | solution.py:19
  216.7 3.5 %bitcast_add_fusion.4 = f32[512,1024]{1,0:T(8,128)} fusion(f32[128,4,1024]{2,0,1:T(8,128)S(1)} %add_add_fusion.2, f32[512,1024]{1,0:T(8,128)} %get-tuple-element.124, pred[]{:T(512)S(6)} %compare.11), kind=kLoop, calls=%fused_computation.5.clone.1 | loop fusion | flops 1048576 | bytes 6291457 | tf_op jit(solution)/shard_map/while/body/eval_jaxpr/add | solution.py:134
  220.2 3.0 %copy.108 = f32[512,1024]{0,1:T(8,128)} copy(f32[512,1024]{1,0:T(8,128)} %get-tuple-element.32) | data formatting | bytes 4194304 | tf_op jit(solution)/shard_map/while | solution.py:136
  (148 shorter events, 73.5 us)
Async XLA Ops:
  6.5 0.7 copy-start
  6.5 107.6 %all-gather.2.cloned.1.call-start = ((), (), s32[]{:S(2)}) async-start(), calls=%async_computation.2 | async-start | bytes 11796480 | tf_op jit(solution)/shard_map/all_gather | solution.py:129
  8.6 1.0 copy-start.5
  15.0 0.8 copy-start.8
  15.0 1.0 copy-start.9
  15.0 8.2 %copy-start.4 = (bf16[1,1,16,256,256]{4,3,2,1,0:T(8,128)(2,1)S(1)}, bf16[1,1,16,256,256]{4,3,2,1,0:T(8,128)(2,1)}, u32[]{:S(2)}) copy-start(bf16[1,1,16,256,256]{4,3,2,1,0:T(8,128)(2,1)} %param.12) | copy-start | bytes 6291460
  16.9 11.9 %all-to-all-start = ((bf16[8,1,2]{2,1,0:T(2,128)(2,1)}), bf16[8,1,2]{2,1,0:T(2,128)(2,1)S(1)}, u32[]{:S(2)}, u32[]{:S(2)}) async-start(bf16[8,1,2]{2,1,0:T(2,128)(2,1)} %all_to_all.12), calls=%async_computation | async-start | bytes 8192 | tf_op jit(solution)/shard_map/all_to_all | solution.py:91
  27.5 5.9 %copy-start.10 = (bf16[1,2,25]{2,1,0:T(2,128)(2,1)S(1)}, bf16[1,2,25]{2,1,0:T(2,128)(2,1)}, u32[]{:S(2)}) copy-start(bf16[1,2,25]{2,1,0:T(2,128)(2,1)} %param.21) | copy-start | bytes 304
  28.8 53.4 %all-to-all-start.1 = ((bf16[8,2,65536]{2,1,0:T(2,128)(2,1)}), bf16[8,2,65536]{2,1,0:T(2,128)(2,1)}, u32[]{:S(2)}, u32[]{:S(2)}) async-start(bf16[8,2,65536]{2,1,0:T(2,128)(2,1)} %reshape.132), calls=%async_computation.1 | async-start | bytes 4194304 | tf_op jit(solution)/shard_map/all_to_all | solution.py:90
  33.4 2.1 copy-start.6
  33.4 2.1 copy-start.7
  33.4 2.1 copy-start.11
  220.2 3.0 %copy-start.2 = (f32[512,1024]{0,1:T(8,128)S(1)}, f32[512,1024]{0,1:T(8,128)}, u32[]{:S(2)}) copy-start(f32[512,1024]{0,1:T(8,128)} %copy.107) | copy-start | bytes 6291460
  230.0 1.2 copy-start.3
  238.2 1.9 copy-start.1
Sparse Core Ops, SparseCore 0:
  15.2 98.9 all-gather.1
